TPU v7x, 128 devices: a whole 4x4x4 slice. The times are simulated.
128 devices in a mesh: row: 16 (over z_hi, y, core), col: 8 (over x, z_lo).
Axes of the slice: x: 4, y: 4, z: 4 (z_hi: 2, z_lo: 2; z = z_hi * 2 + z_lo), core: 2. Of those that a mesh axis runs over, the one named last changes fastest.
Arguments:
- word_topic: bfloat16 [131072, 128], P(('row', 'col')), may hold values from 0.25 to 4
- topic_weight: float32 [128], replicated, may hold values from 0.1 to 10
- tile_blocks: int32 [16, 8, 64, 2], P('row', 'col'), may hold values from 0 to 63, as said below
- tile_live: int32 [16, 8], P('row', 'col'), may hold values from 16 to 64, as said below
- pair_counts: int32 [16, 8, 64, 256, 256], P('row', 'col'), may hold values from 0 to 63
Outputs:
- next_word_topic: bfloat16 [131072, 128], P(('row', 'col'))
- next_topic_weight: float32 [128], replicated
Inputs may be any that keep to these rules, and one draw needn't show every extreme that they name: `tile_blocks`: each entry pair is (a word block among the device's 32 blocks of first words, a word block among its 64 blocks of second words); the slots of one device name distinct tiles. `tile_live`: slots at or beyond a device's count hold no tile; some device fills all slots.
All inputs are finite; a program needn't handle non-finite values.
Results may differ from a plain program's by a relative error of at most 0.0049.
Values may be sent and summed in bfloat16 or wider, within the bound.
No kernel may reach another device: no remote copies, remote signals or barrier semaphores. Data moves between devices by JAX's collectives and lax.ppermute only.
A program may use at most 128 MiB of HBM per device.

v0:
```python
from functools import partial
import jax
import jax.numpy as jnp
from jax import lax
from jax.sharding import PartitionSpec as P

V = 131072
K = 128
BLK = 256
ITERS = 2


def group_step(
    left_blocks, right_blocks, blocks, tiles_all, live, want_row, want_col, group, carry
):
    tile_group = 8
    start = group * tile_group
    row_ids = lax.dynamic_slice_in_dim(blocks[:, 0], start, tile_group)
    col_ids = lax.dynamic_slice_in_dim(blocks[:, 1], start, tile_group)
    tiles = lax.dynamic_slice_in_dim(tiles_all, start, tile_group, 0)
    alive = start + jnp.arange(tile_group, dtype=jnp.int32) < live
    left = left_blocks[row_ids]
    right = right_blocks[col_ids]
    denoms = jnp.einsum("gak,gbk->gab", left, right, preferred_element_type=jnp.float32)
    ratio = jnp.where(alive[:, None, None], tiles.astype(jnp.float32) / denoms, 0.0).astype(
        jnp.bfloat16
    )
    results = []
    place = 0
    row_part = jnp.einsum("gab,gbk->gak", ratio, right, preferred_element_type=jnp.float32)
    results.append(carry[place].at[row_ids].add(row_part))
    place = place + 1
    col_part = jnp.einsum("gab,gak->gbk", ratio, left, preferred_element_type=jnp.float32)
    results.append(carry[place].at[col_ids].add(col_part))
    return tuple(results)


def sweep(left_blocks, right_blocks, blocks, tiles_all, live):
    starts = []
    starts.append(jnp.zeros(left_blocks.shape, jnp.float32))
    starts.append(jnp.zeros(right_blocks.shape, jnp.float32))
    stepper = partial(group_step, left_blocks, right_blocks, blocks, tiles_all, live, True, True)
    turns = (live + 7) // 8
    return lax.fori_loop(0, turns, stepper, tuple(starts))


def local(word_topic, topic_weight, tile_blocks, tile_live, pair_counts):
    blocks = tile_blocks[0, 0]
    live = tile_live[0, 0]
    tiles_all = pair_counts[0, 0]
    weights = word_topic
    shares = topic_weight
    for step in range(ITERS):
        row_phi = lax.all_gather(weights, "col", axis=0, tiled=True)
        col_phi = lax.all_gather(weights, "row", axis=0, tiled=True)
        scaled = (row_phi.astype(jnp.float32) * shares).astype(jnp.bfloat16)
        left_blocks = scaled.reshape(-1, BLK, K)
        right_blocks = col_phi.reshape(-1, BLK, K)
        row_acc, col_acc = sweep(left_blocks, right_blocks, blocks, tiles_all, live)
        row_terms = row_acc.reshape(-1, K)
        col_terms = col_acc.reshape(-1, K)
        row_sum = lax.psum_scatter(row_terms, "col", scatter_dimension=0, tiled=True)
        col_sum = lax.psum_scatter(col_terms, "row", scatter_dimension=0, tiled=True)
        expected = weights.astype(jnp.float32) * (shares * row_sum + col_sum)
        totals = lax.psum(jnp.sum(expected, axis=0), ("row", "col"))
        weights = (V * expected / totals).astype(jnp.bfloat16)
        shares = K * totals / jnp.sum(totals)
    return (weights, shares)


def solution(mesh):
    in_specs = (
        P(("row", "col"), None),
        P(),
        P("row", "col", None, None),
        P("row", "col"),
        P("row", "col", None, None, None),
    )
    out_specs = (P(("row", "col"), None), P())
    return jax.shard_map(local, mesh=mesh, in_specs=in_specs, out_specs=out_specs, check_vma=False)
```

profile of v0, /device:TPU:1, one launch (start us, length us, event | category | flops | bytes accessed | tf_op | source)
XLA Modules:
  0.0 1029.4 jit_solution(16607636807630387287)
XLA Ops:
  9.4 52.8 %all-gather.5.cloned.1.call-done = bf16[8192,128]{1,0:T(8,128)(2,1)} async-done(((bf16[1024,128]{1,0:T(8,128)(2,1)}), bf16[8192,128]{1,0:T(8,128)(2,1)}) %all-gather.5.cloned.1.call-update) | async-done | bytes 2097168 | tf_op jit(solution)/shard_map/all_gather | solution.py:54
  62.1 3.3 multiply_convert_fusion.1
  65.5 57.8 %all-gather.7.cloned.1.call-done = bf16[16384,128]{1,0:T(8,128)(2,1)} async-done(((bf16[1024,128]{1,0:T(8,128)(2,1)}), bf16[16384,128]{1,0:T(8,128)(2,1)}) %all-gather.7.cloned.1.call-update) | async-done | bytes 4194320 | tf_op jit(solution)/shard_map/all_gather | solution.py:55
  123.3 4.2 broadcast.60.clone
  130.0 108.6 %while.24 = (s32[]{:T(128)}, f32[32,256,128]{2,1,0:T(8,128)}, f32[64,256,128]{2,1,0:T(8,128)}, s32[]{:T(128)}, s32[64,2]{0,1:T(2,128)S(1)}, /*index=5*/s32[]{:T(...) while((s32[]{:T(128)}, f32[32,256,128]{2,1,0:T(8,128)}, ...), condition=%wide.region_3.4_spmd, body=%wide.region_0.3_spmd.sunk | while | flops 405276736 | bytes 17835532 | solution.py:44
  132.4 2.8 gather_fusion.1
  138.4 3.4 scatter_fusion.1
  142.3 3.3 scatter_fusion
  148.0 2.8 gather_fusion.1
  154.1 3.3 scatter_fusion.1
  157.8 3.3 scatter_fusion
  169.5 3.3 scatter_fusion.1
  173.3 3.3 scatter_fusion
  185.0 3.4 scatter_fusion.1
  188.8 3.3 scatter_fusion
  200.5 3.3 scatter_fusion.1
  204.2 3.3 scatter_fusion
  216.0 3.4 scatter_fusion.1
  219.8 3.3 scatter_fusion
  231.5 3.4 scatter_fusion.1
  235.3 3.4 scatter_fusion
  239.3 103.5 %reduce-scatter.5.cloned.1.call-done = f32[1024,128]{1,0:T(8,128)} async-done(((f32[8192,128]{1,0:T(8,128)}), f32[1024,128]{1,0:T(8,128)}) %reduce-scatter.5.cloned.1.call-update) | async-done | bytes 524304 | tf_op jit(solution)/shard_map/reduce_scatter | solution.py:62
  342.8 106.7 %reduce-scatter.7.cloned.1.call-done = f32[1024,128]{1,0:T(8,128)} async-done(((f32[16384,128]{1,0:T(8,128)}), f32[1024,128]{1,0:T(8,128)}) %reduce-scatter.7.cloned.1.call-update) | async-done | bytes 524304 | tf_op jit(solution)/shard_map/reduce_scatter | solution.py:63
  450.9 65.3 %psum.14 = f32[128]{0:T(128)S(1)} all-reduce(f32[128]{0:T(128)S(1)} %fusion.4), channel_id=1, replica_groups=mesh['row'=16,'col'=8] {'row','col'}, use_global_device_ids=true, to_apply=%region_7.8 | all-reduce | flops 128 | bytes 1024 | tf_op jit(solution)/shard_map/psum | solution.py:65
  520.1 43.9 %all-gather.9.cloned.1.call-done = bf16[8192,128]{1,0:T(8,128)(2,1)} async-done(((bf16[1024,128]{1,0:T(8,128)(2,1)}), bf16[8192,128]{1,0:T(8,128)(2,1)}) %all-gather.9.cloned.1.call-update) | async-done | bytes 2097168 | tf_op jit(solution)/shard_map/all_gather | solution.py:54
  564.1 3.3 multiply_convert_fusion
  567.4 58.3 %all-gather.11.cloned.1.call-done = bf16[16384,128]{1,0:T(8,128)(2,1)} async-done(((bf16[1024,128]{1,0:T(8,128)(2,1)}), bf16[16384,128]{1,0:T(8,128)(2,1)}) %all-gather.11.cloned.1.call-update) | async-done | bytes 4194320 | tf_op jit(solution)/shard_map/all_gather | solution.py:55
  625.7 4.2 broadcast.60
  632.4 108.6 %while.25 = (s32[]{:T(128)}, f32[32,256,128]{2,1,0:T(8,128)}, f32[64,256,128]{2,1,0:T(8,128)}, s32[]{:T(128)}, s32[64,2]{0,1:T(2,128)S(1)}, /*index=5*/s32[]{:T(...) while((s32[]{:T(128)}, f32[32,256,128]{2,1,0:T(8,128)}, ...), condition=%wide.region_12.13_spmd, body=%wide.region_9.12_spmd.sunk | while | flops 405276736 | bytes 17835532 | solution.py:44
  640.8 3.4 scatter_fusion.3
  644.6 3.3 scatter_fusion.2
  656.4 3.3 scatter_fusion.3
  660.2 3.3 scatter_fusion.2
  671.9 3.3 scatter_fusion.3
  675.6 3.3 scatter_fusion.2
  687.4 3.4 scatter_fusion.3
  691.2 3.3 scatter_fusion.2
  696.8 2.8 gather_fusion.3
  702.9 3.3 scatter_fusion.3
  706.6 3.3 scatter_fusion.2
  712.3 2.8 gather_fusion.3
  718.4 3.4 scatter_fusion.3
  722.2 3.3 scatter_fusion.2
  733.9 3.4 scatter_fusion.3
  737.7 3.4 scatter_fusion.2
  741.8 103.4 %reduce-scatter.9.cloned.1.call-done = f32[1024,128]{1,0:T(8,128)} async-done(((f32[8192,128]{1,0:T(8,128)}), f32[1024,128]{1,0:T(8,128)}) %reduce-scatter.9.cloned.1.call-update) | async-done | bytes 524304 | tf_op jit(solution)/shard_map/reduce_scatter | solution.py:62
  845.2 106.7 %reduce-scatter.11.cloned.1.call-done = f32[1024,128]{1,0:T(8,128)} async-done(((f32[16384,128]{1,0:T(8,128)}), f32[1024,128]{1,0:T(8,128)}) %reduce-scatter.11.cloned.1.call-update) | async-done | bytes 524304 | tf_op jit(solution)/shard_map/reduce_scatter | solution.py:63
  953.2 65.5 %psum.15 = f32[128]{0:T(128)S(1)} all-reduce(f32[128]{0:T(128)S(1)} %fusion.5), channel_id=1, replica_groups=mesh['row'=16,'col'=8] {'row','col'}, use_global_device_ids=true, to_apply=%region_16.17 | all-reduce | flops 128 | bytes 1024 | tf_op jit(solution)/shard_map/psum | solution.py:65
  (170 shorter events, 130.1 us)
Async XLA Ops:
  7.2 55.0 %all-gather.5.cloned.1.call-start = ((), (), s32[]{:S(2)}) async-start(), calls=%async_computation.4 | async-start | bytes 2359296 | tf_op jit(solution)/shard_map/all_gather | solution.py:54
  7.9 115.4 %all-gather.7.cloned.1.call-start = ((), (), s32[]{:S(2)}) async-start(), calls=%async_computation.5 | async-start | bytes 4456448 | tf_op jit(solution)/shard_map/all_gather | solution.py:55
  8.6 334.2 %reduce-scatter.5.cloned.1.call-start = ((), (), s32[]{:S(2)}) async-start(), calls=%async_computation.6 | async-start | bytes 4718592 | tf_op jit(solution)/shard_map/reduce_scatter | solution.py:62
  127.6 2.5 copy-start.2
  238.7 210.9 %reduce-scatter.7.cloned.1.call-start = ((), (), s32[]{:S(2)}) async-start(), calls=%async_computation.7 | async-start | bytes 8912896 | tf_op jit(solution)/shard_map/reduce_scatter | solution.py:63
  238.7 210.8 %copy-start.1 = (bf16[1024,128]{1,0:T(8,128)(2,1)S(1)}, bf16[1024,128]{1,0:T(8,128)(2,1)}, u32[]{:S(2)}) copy-start(bf16[1024,128]{1,0:T(8,128)(2,1)} %param.9) | copy-start | bytes 786436
  238.7 210.8 %copy-start.3 = (f32[128]{0:T(128)S(1)}, f32[128]{0:T(128)}, u32[]{:S(2)}) copy-start(f32[128]{0:T(128)} %param.10) | copy-start | bytes 1540
  239.3 324.8 %all-gather.9.cloned.1.call-start = ((), (), s32[]{:S(2)}) async-start(), calls=%async_computation.8 | async-start | bytes 2359296 | tf_op jit(solution)/shard_map/all_gather | solution.py:54
  518.2 107.5 %all-gather.11.cloned.1.call-start = ((), (), s32[]{:S(2)}) async-start(), calls=%async_computation.9 | async-start | bytes 4456448 | tf_op jit(solution)/shard_map/all_gather | solution.py:55
  518.8 326.4 %reduce-scatter.9.cloned.1.call-start = ((), (), s32[]{:S(2)}) async-start(), calls=%async_computation.10 | async-start | bytes 4718592 | tf_op jit(solution)/shard_map/reduce_scatter | solution.py:62
  741.0 210.8 %reduce-scatter.11.cloned.1.call-start = ((), (), s32[]{:S(2)}) async-start(), calls=%async_computation.11 | async-start | bytes 8912896 | tf_op jit(solution)/shard_map/reduce_scatter | solution.py:63
  741.1 210.8 %copy-start = (bf16[1024,128]{1,0:T(8,128)(2,1)S(1)}, bf16[1024,128]{1,0:T(8,128)(2,1)}, u32[]{:S(2)}) copy-start(bf16[1024,128]{1,0:T(8,128)(2,1)} %divide_convert_fusion.1) | copy-start | bytes 786436
Sparse Core Ops, SparseCore 0:
  9.6 52.4 all-gather.4
  64.6 58.7 all-gather.6
  238.8 103.9 reduce-scatter.4
  347.0 102.4 reduce-scatter.6
  518.3 45.6 all-gather.8
  566.9 58.7 all-gather.10
  741.2 103.9 reduce-scatter.8
  849.5 102.2 reduce-scatter.10
where the time goes:
time: 1030 us
  waiting for transfers between devices  636 us (62%)
  blocking collectives  131 us (13%)
  other arithmetic  120 us (12%)
  local copies, waits for them, and re-layouts  84.5 us (8%)
  matrix products  41.8 us (4%)
  between operations  14.8 us (1%)
    reduce_scatter x2, waiting for transfers between devices, local(): lax.psum_scatter(col_terms, 'row', scatter_dimension=0, tiled=True)  213 us
    reduce_scatter x2, waiting for transfers between devices, local(): lax.psum_scatter(row_terms, 'col', scatter_dimension=0, tiled=True)  207 us
    psum x2, blocking collectives, local(): totals = lax.psum(jnp.sum(expected, axis=0), ('row', 'col'))  131 us
    all_gather x2, waiting for transfers between devices, local(): col_phi = lax.all_gather(weights, 'row', axis=0, tiled=True)  116 us
    all_gather x2, waiting for transfers between devices, local(): row_phi = lax.all_gather(weights, 'col', axis=0, tiled=True)  96.7 us
    scatter-add x14, other arithmetic, group_step(): results.append(carry[place].at[col_ids].add(col_part))  46.9 us
    scatter-add x14, other arithmetic, group_step(): results.append(carry[place].at[row_ids].add(row_part))  46.4 us
    gather x14, local copies, waits for them, and re-layouts, group_step(): right = right_blocks[col_ids]  39.7 us
  transfers between devices with their start and end apart: 8, of which 8 were waited for; matrix products, arithmetic and copies ran while one was open for 1% of the time, Pallas kernels for 0%

commit v1 on v0

--- a/solution.py
+++ b/solution.py
@@ -62,7 +62,9 @@
         row_sum = lax.psum_scatter(row_terms, "col", scatter_dimension=0, tiled=True)
         col_sum = lax.psum_scatter(col_terms, "row", scatter_dimension=0, tiled=True)
         expected = weights.astype(jnp.float32) * (shares * row_sum + col_sum)
-        totals = lax.psum(jnp.sum(expected, axis=0), ("row", "col"))
+        block = jnp.sum(expected, axis=0)
+        parts = lax.all_gather(block, ("row", "col"), axis=0, tiled=False)
+        totals = parts.sum(axis=0)
         weights = (V * expected / totals).astype(jnp.bfloat16)
         shares = K * totals / jnp.sum(totals)
     return (weights, shares)

time: 1030 us -> 1520 us (1.48)
  blocking collectives: 131 us -> 592 us
    all_gather x0 -> x2, blocking collectives: none -> 592 us  [local(): parts = lax.all_gather(block, ('row', 'col'), axis=0, tiled=False)]
    psum x2 -> x0, blocking collectives: 131 us -> none  [local(): totals = lax.psum(jnp.sum(expected, axis=0), ('row', 'col'))]
  transfers between devices with their start and end apart: 8 -> 8, of which waited for: 8 -> 8; matrix products, arithmetic and copies ran while one was open for 1% -> 0% of each run, Pallas kernels for 0% -> 0%
where the time goes in v1:
time: 1520 us; the launch traced here: 1500 us
  waiting for transfers between devices  650 us (43%)
  blocking collectives  592 us (39%)
  other arithmetic  120 us (8%)
  local copies, waits for them, and re-layouts  84.5 us (6%)
  matrix products  41.8 us (3%)
    all_gather x2, blocking collectives, local(): parts = lax.all_gather(block, ('row', 'col'), axis=0, tiled=False)  592 us
    reduce_scatter x2, waiting for transfers between devices, local(): lax.psum_scatter(col_terms, 'row', scatter_dimension=0, tiled=True)  213 us
    reduce_scatter x2, waiting for transfers between devices, local(): lax.psum_scatter(row_terms, 'col', scatter_dimension=0, tiled=True)  207 us
    all_gather x2, waiting for transfers between devices, local(): col_phi = lax.all_gather(weights, 'row', axis=0, tiled=True)  116 us
    all_gather x2, waiting for transfers between devices, local(): row_phi = lax.all_gather(weights, 'col', axis=0, tiled=True)  110 us
    scatter-add x14, other arithmetic, group_step(): results.append(carry[place].at[col_ids].add(col_part))  46.9 us
    scatter-add x14, other arithmetic, group_step(): results.append(carry[place].at[row_ids].add(row_part))  46.4 us
    gather x14, local copies, waits for them, and re-layouts, group_step(): right = right_blocks[col_ids]  39.7 us
  transfers between devices with their start and end apart: 8, of which 8 were waited for; matrix products, arithmetic and copies ran while one was open for 0% of the time, Pallas kernels for 0%

profile of v1, /device:TPU:1, one launch (start us, length us, event | category | flops | bytes accessed | tf_op | source)
XLA Modules:
  0.0 1504.5 jit_solution(14512551274146057220)
XLA Ops:
  9.4 52.8 %all-gather.9.cloned.1.call-done = bf16[8192,128]{1,0:T(8,128)(2,1)} async-done(((bf16[1024,128]{1,0:T(8,128)(2,1)}), bf16[8192,128]{1,0:T(8,128)(2,1)}) %all-gather.9.cloned.1.call-update) | async-done | bytes 2097168 | tf_op jit(solution)/shard_map/all_gather | solution.py:54
  62.1 3.3 multiply_convert_fusion.1
  65.5 57.8 %all-gather.11.cloned.1.call-done = bf16[16384,128]{1,0:T(8,128)(2,1)} async-done(((bf16[1024,128]{1,0:T(8,128)(2,1)}), bf16[16384,128]{1,0:T(8,128)(2,1)}) %all-gather.11.cloned.1.call-update) | async-done | bytes 4194320 | tf_op jit(solution)/shard_map/all_gather | solution.py:55
  123.3 4.2 broadcast.67.clone
  130.0 108.6 %while.24 = (s32[]{:T(128)}, f32[32,256,128]{2,1,0:T(8,128)}, f32[64,256,128]{2,1,0:T(8,128)}, s32[]{:T(128)}, s32[64,2]{0,1:T(2,128)S(1)}, /*index=5*/s32[]{:T(...) while((s32[]{:T(128)}, f32[32,256,128]{2,1,0:T(8,128)}, ...), condition=%wide.region_3.4_spmd, body=%wide.region_0.3_spmd.sunk | while | flops 405276736 | bytes 17835532 | solution.py:44
  132.4 2.8 gather_fusion.1
  138.4 3.4 scatter_fusion.1
  142.3 3.3 scatter_fusion
  148.0 2.8 gather_fusion.1
  154.1 3.3 scatter_fusion.1
  157.8 3.3 scatter_fusion
  163.5 2.8 gather_fusion.1
  169.5 3.3 scatter_fusion.1
  173.3 3.3 scatter_fusion
  185.0 3.4 scatter_fusion.1
  188.8 3.3 scatter_fusion
  200.5 3.3 scatter_fusion.1
  204.2 3.3 scatter_fusion
  216.0 3.4 scatter_fusion.1
  219.8 3.3 scatter_fusion
  231.5 3.4 scatter_fusion.1
  235.3 3.4 scatter_fusion
  239.3 103.5 %reduce-scatter.5.cloned.1.call-done = f32[1024,128]{1,0:T(8,128)} async-done(((f32[8192,128]{1,0:T(8,128)}), f32[1024,128]{1,0:T(8,128)}) %reduce-scatter.5.cloned.1.call-update) | async-done | bytes 524304 | tf_op jit(solution)/shard_map/reduce_scatter | solution.py:62
  342.8 106.7 %reduce-scatter.7.cloned.1.call-done = f32[1024,128]{1,0:T(8,128)} async-done(((f32[16384,128]{1,0:T(8,128)}), f32[1024,128]{1,0:T(8,128)}) %reduce-scatter.7.cloned.1.call-update) | async-done | bytes 524304 | tf_op jit(solution)/shard_map/reduce_scatter | solution.py:63
  450.9 296.0 %all-gather.2 = f32[128,1,128]{2,1,0:T(1,128)S(1)} all-gather(f32[1,1,128]{2,1,0:T(1,128)S(1)} %bitcast.69), channel_id=2, replica_groups=mesh['row'=16,'col'=8] {'row','col'}, dimensions={0}, use_global_device_ids=true | all-gather | bytes 66048 | tf_op jit(solution)/shard_map/all_gather | solution.py:66
  751.0 57.3 %all-gather.13.cloned.1.call-done = bf16[8192,128]{1,0:T(8,128)(2,1)} async-done(((bf16[1024,128]{1,0:T(8,128)(2,1)}), bf16[8192,128]{1,0:T(8,128)(2,1)}) %all-gather.13.cloned.1.call-update) | async-done | bytes 2097168 | tf_op jit(solution)/shard_map/all_gather | solution.py:54
  808.3 3.3 multiply_convert_fusion
  811.7 58.3 %all-gather.15.cloned.1.call-done = bf16[16384,128]{1,0:T(8,128)(2,1)} async-done(((bf16[1024,128]{1,0:T(8,128)(2,1)}), bf16[16384,128]{1,0:T(8,128)(2,1)}) %all-gather.15.cloned.1.call-update) | async-done | bytes 4194320 | tf_op jit(solution)/shard_map/all_gather | solution.py:55
  870.0 4.2 broadcast.67
  876.7 108.6 %while.25 = (s32[]{:T(128)}, f32[32,256,128]{2,1,0:T(8,128)}, f32[64,256,128]{2,1,0:T(8,128)}, s32[]{:T(128)}, s32[64,2]{0,1:T(2,128)S(1)}, /*index=5*/s32[]{:T(...) while((s32[]{:T(128)}, f32[32,256,128]{2,1,0:T(8,128)}, ...), condition=%wide.region_12.13_spmd, body=%wide.region_9.12_spmd.sunk | while | flops 405276736 | bytes 17835532 | solution.py:44
  885.1 3.4 scatter_fusion.3
  888.9 3.3 scatter_fusion.2
  894.6 2.8 gather_fusion.3
  900.7 3.3 scatter_fusion.3
  904.5 3.3 scatter_fusion.2
  916.2 3.3 scatter_fusion.3
  919.9 3.3 scatter_fusion.2
  931.7 3.4 scatter_fusion.3
  935.5 3.3 scatter_fusion.2
  947.2 3.3 scatter_fusion.3
  950.9 3.3 scatter_fusion.2
  962.6 3.4 scatter_fusion.3
  966.5 3.3 scatter_fusion.2
  978.1 3.4 scatter_fusion.3
  982.0 3.4 scatter_fusion.2
  986.1 103.4 %reduce-scatter.9.cloned.1.call-done = f32[1024,128]{1,0:T(8,128)} async-done(((f32[8192,128]{1,0:T(8,128)}), f32[1024,128]{1,0:T(8,128)}) %reduce-scatter.9.cloned.1.call-update) | async-done | bytes 524304 | tf_op jit(solution)/shard_map/reduce_scatter | solution.py:62
  1089.5 106.6 %reduce-scatter.11.cloned.1.call-done = f32[1024,128]{1,0:T(8,128)} async-done(((f32[16384,128]{1,0:T(8,128)}), f32[1024,128]{1,0:T(8,128)}) %reduce-scatter.11.cloned.1.call-update) | async-done | bytes 524304 | tf_op jit(solution)/shard_map/reduce_scatter | solution.py:63
  1197.5 296.2 %all-gather.3 = f32[128,1,128]{2,1,0:T(1,128)S(1)} all-gather(f32[1,1,128]{2,1,0:T(1,128)S(1)} %bitcast.70), channel_id=3, replica_groups=mesh['row'=16,'col'=8] {'row','col'}, dimensions={0}, use_global_device_ids=true | all-gather | bytes 66048 | tf_op jit(solution)/shard_map/all_gather | solution.py:66
  (170 shorter events, 130.3 us)
Async XLA Ops:
  7.2 55.0 %all-gather.9.cloned.1.call-start = ((), (), s32[]{:S(2)}) async-start(), calls=%async_computation.4 | async-start | bytes 2359296 | tf_op jit(solution)/shard_map/all_gather | solution.py:54
  7.9 115.4 %all-gather.11.cloned.1.call-start = ((), (), s32[]{:S(2)}) async-start(), calls=%async_computation.5 | async-start | bytes 4456448 | tf_op jit(solution)/shard_map/all_gather | solution.py:55
  8.6 334.2 %reduce-scatter.5.cloned.1.call-start = ((), (), s32[]{:S(2)}) async-start(), calls=%async_computation.6 | async-start | bytes 4718592 | tf_op jit(solution)/shard_map/reduce_scatter | solution.py:62
  127.6 2.5 copy-start.2
  238.7 210.9 %reduce-scatter.7.cloned.1.call-start = ((), (), s32[]{:S(2)}) async-start(), calls=%async_computation.7 | async-start | bytes 8912896 | tf_op jit(solution)/shard_map/reduce_scatter | solution.py:63
  238.7 210.8 %copy-start.1 = (bf16[1024,128]{1,0:T(8,128)(2,1)S(1)}, bf16[1024,128]{1,0:T(8,128)(2,1)}, u32[]{:S(2)}) copy-start(bf16[1024,128]{1,0:T(8,128)(2,1)} %param.9) | copy-start | bytes 786436
  238.7 210.8 %copy-start.3 = (f32[128]{0:T(128)S(1)}, f32[128]{0:T(128)}, u32[]{:S(2)}) copy-start(f32[128]{0:T(128)} %param.10) | copy-start | bytes 1540
  239.3 569.1 %all-gather.13.cloned.1.call-start = ((), (), s32[]{:S(2)}) async-start(), calls=%async_computation.8 | async-start | bytes 2359296 | tf_op jit(solution)/shard_map/all_gather | solution.py:54
  749.7 120.2 %all-gather.15.cloned.1.call-start = ((), (), s32[]{:S(2)}) async-start(), calls=%async_computation.9 | async-start | bytes 4456448 | tf_op jit(solution)/shard_map/all_gather | solution.py:55
  750.3 339.2 %reduce-scatter.9.cloned.1.call-start = ((), (), s32[]{:S(2)}) async-start(), calls=%async_computation.10 | async-start | bytes 4718592 | tf_op jit(solution)/shard_map/reduce_scatter | solution.py:62
  985.3 210.8 %reduce-scatter.11.cloned.1.call-start = ((), (), s32[]{:S(2)}) async-start(), calls=%async_computation.11 | async-start | bytes 8912896 | tf_op jit(solution)/shard_map/reduce_scatter | solution.py:63
  985.4 210.7 %copy-start = (bf16[1024,128]{1,0:T(8,128)(2,1)S(1)}, bf16[1024,128]{1,0:T(8,128)(2,1)}, u32[]{:S(2)}) copy-start(bf16[1024,128]{1,0:T(8,128)(2,1)} %divide_convert_fusion.1) | copy-start | bytes 786436
Sparse Core Ops, SparseCore 0:
  9.6 52.4 all-gather.8
  64.6 58.7 all-gather.10
  238.8 103.9 reduce-scatter.4
  347.0 102.4 reduce-scatter.6
  749.9 58.4 all-gather.12
  811.2 58.7 all-gather.14
  985.4 103.9 reduce-scatter.8
  1093.8 102.2 reduce-scatter.10
